TPU v7x, 128 devices: a whole 4x4x4 slice. The times are simulated.
128 devices in a mesh: row: 16 (over z, y_hi, core), col: 8 (over y_lo, x).
Axes of the slice: x: 4, y: 4 (y_hi: 2, y_lo: 2; y = y_hi * 2 + y_lo), z: 4, core: 2. Of those that a mesh axis runs over, the one named last changes fastest.
Arguments:
- layer_input: bfloat16 [2, 8192, 1024], P(None, 'row', 'col'), may hold values from -96 to 96
- out_grad: bfloat16 [2, 8192, 1024], P(None, 'row', 'col'), may hold values from -6 to 6
- token_route: int32 [2, 8192], P(None, 'row'), may hold values from 0 to 8191, as said below
- seq_lengths: int32 [2, 16, 4], P(None, 'row'), may hold values from 0 to 512, as said below
- positions: int32 [2, 8192], P(None, 'row'), may hold values from 0 to 3580, as said below
- attn_gain: bfloat16 [1024], replicated, may hold values from 0.099609375 to 1.8984375
- query_weight: bfloat16 [1024, 2048], P('row', 'col'), may hold values from -0.1875 to 0.1875
- key_weight: bfloat16 [1024, 1024], P('row', 'col'), may hold values from -0.1875 to 0.1875
- value_weight: bfloat16 [1024, 1024], P('row', 'col'), may hold values from -0.1875 to 0.1875
- query_gain: bfloat16 [128], replicated, may hold values from 0.099609375 to 1.8984375
- key_gain: bfloat16 [128], replicated, may hold values from 0.099609375 to 1.8984375
- out_weight: bfloat16 [2048, 1024], P('col', 'row'), may hold values from -0.5 to 0.5
- mlp_gain: bfloat16 [1024], replicated, may hold values from 0.099609375 to 1.8984375
- gate_weight: bfloat16 [1024, 3072], P('row', 'col'), may hold values from -0.1875 to 0.1875
- up_weight: bfloat16 [1024, 3072], P('row', 'col'), may hold values from -0.1875 to 0.1875
- down_weight: bfloat16 [3072, 1024], P('col', 'row'), may hold values from -0.109375 to 0.109375
Outputs:
- layer_output: bfloat16 [2, 8192, 1024], P(None, 'row', 'col')
- input_grad: bfloat16 [2, 8192, 1024], P(None, 'row', 'col')
- attn_gain_grad: float32 [1024], replicated
- query_grad: float32 [1024, 2048], P('row', 'col')
- key_grad: float32 [1024, 1024], P('row', 'col')
- value_grad: float32 [1024, 1024], P('row', 'col')
- query_gain_grad: float32 [128], replicated
- key_gain_grad: float32 [128], replicated
- out_proj_grad: float32 [2048, 1024], P('col', 'row')
- mlp_gain_grad: float32 [1024], replicated
- gate_grad: float32 [1024, 3072], P('row', 'col')
- up_grad: float32 [1024, 3072], P('row', 'col')
- down_grad: float32 [3072, 1024], P('col', 'row')
Inputs may be any that keep to these rules, and one draw needn't show every extreme that they name: Each row of token_route holds every number from 0 to 8191 once. Each aligned block of 512 entries holds the same number of entries of every group (g * 512 to (g + 1) * 512 - 1). `seq_lengths`: each row of 4 lengths sums to 512; nonzero lengths come first and zeros mark unused slots. Some row holds a single sequence of 512 tokens. Within each sequence of the group layout, positions rise by 1 to 3 from one token to the next.
All inputs are finite; a program needn't handle non-finite values.
Results may differ from a plain program's by a relative error of at most 0.018.
Values may be sent and summed in bfloat16 or wider, within the bound.
No kernel may reach another device: no remote copies, remote signals or barrier semaphores. Data moves between devices by JAX's collectives and lax.ppermute only.
A program may use at most 128 MiB of HBM per device.

v0:
```python
import math

import jax
import jax.numpy as jnp
from jax import lax
from jax.sharding import PartitionSpec as P

D = 1024
HEAD_SIZE = 128


EPSILON = 1e-06
ROPE_BASE = 1000000.0
NEGATIVE = -1e30
row_block = 512


def project(left_side, right_side):
    return jnp.dot(left_side, right_side, preferred_element_type=jnp.float32)


def project_back(left_side, right_side):
    return lax.dot_general(
        left_side, right_side, (((1,), (1,)), ((), ())), preferred_element_type=jnp.float32
    )


def weight_term(left_side, right_side):
    return lax.dot_general(
        left_side, right_side, (((0,), (0,)), ((), ())), preferred_element_type=jnp.float32
    )


def rotate(tensor):
    half_size = tensor.shape[-1] // 2
    return jnp.concatenate([-tensor[..., half_size:], tensor[..., :half_size]], axis=-1)


def unrotate(tensor):
    half_size = tensor.shape[-1] // 2
    return jnp.concatenate([tensor[..., half_size:], -tensor[..., :half_size]], axis=-1)


def rope_tables(position):
    freq_steps = jnp.arange(0, HEAD_SIZE, 2).astype(jnp.float32) / HEAD_SIZE
    frequency = 1.0 / ROPE_BASE**freq_steps
    angles = position.astype(jnp.float32)[:, None] * frequency[None, :]
    angles = jnp.concatenate([angles, angles], axis=-1)
    return (jnp.cos(angles), jnp.sin(angles))


def segment_ids(lengths, group_rows):
    bounds = jnp.cumsum(lengths)[:-1]
    places = jnp.arange(group_rows, dtype=jnp.int32)
    return jnp.sum((places[:, None] >= bounds[None, :]).astype(jnp.int32), axis=1)


def pick_rows(table, index):
    return jax.vmap(lambda rows_in, rows_at: jnp.take(rows_in, rows_at, axis=0))(table, index)


def block_scores(query_rows, key_rows, row_mask):
    raw_scores = jnp.einsum(
        "qkrd,tkd->krqt", query_rows, key_rows, preferred_element_type=jnp.float32
    ) * (1.0 / math.sqrt(HEAD_SIZE))
    return jnp.where(row_mask[None, None], raw_scores, NEGATIVE)


def sum_whole(partial_value):
    return lax.psum(partial_value, "col")


def body(
    layer_input,
    out_grad,
    token_route,
    seq_lengths,
    positions,
    attn_gain,
    query_weight,
    key_weight,
    value_weight,
    query_gain,
    key_gain,
    out_weight,
    mlp_gain,
    gate_weight,
    up_weight,
    down_weight,
):
    row_size = lax.axis_size("row")
    col_index = lax.axis_index("col")
    micro_count = layer_input.shape[0]
    group_rows = layer_input.shape[1]
    width_part = layer_input.shape[2]
    piece_rows = group_rows // row_size
    my_start = col_index * width_part
    route_order = jnp.argsort(token_route, axis=1)
    given_rank = jnp.argsort(route_order, axis=1)
    sorted_route = pick_rows(token_route, route_order)
    slots_out = (sorted_route % group_rows).reshape(micro_count, row_size, piece_rows)
    slots_in = lax.all_to_all(slots_out, "row", split_axis=1, concat_axis=1, tiled=True).reshape(
        micro_count, group_rows
    )
    sent_input = pick_rows(layer_input, route_order).reshape(
        micro_count, row_size, piece_rows, width_part
    )
    sent_grad = pick_rows(out_grad, route_order).reshape(
        micro_count, row_size, piece_rows, width_part
    )
    recv_input, recv_grad = (
        lax.all_to_all(sent_input, "row", split_axis=1, concat_axis=1, tiled=True),
        lax.all_to_all(sent_grad, "row", split_axis=1, concat_axis=1, tiled=True),
    )
    slot_order = jnp.argsort(slots_in, axis=1)
    group_input = pick_rows(recv_input.reshape(micro_count, group_rows, width_part), slot_order)
    group_grad = pick_rows(recv_grad.reshape(micro_count, group_rows, width_part), slot_order)
    gain_one = attn_gain.astype(jnp.float32)
    gain_two = mlp_gain.astype(jnp.float32)
    query_scale = query_gain.astype(jnp.float32)
    key_scale = key_gain.astype(jnp.float32)
    column_mask = (jnp.arange(D) // width_part == col_index).astype(jnp.float32)
    places = jnp.arange(group_rows, dtype=jnp.int32)
    block_size = min(row_block, group_rows)
    grad_totals = [
        jnp.zeros(weight_item.shape, jnp.float32)
        for weight_item in (
            query_weight,
            key_weight,
            value_weight,
            out_weight,
            gate_weight,
            up_weight,
            down_weight,
        )
    ]
    attn_gain_sum = jnp.zeros((D,), jnp.float32)
    mlp_gain_sum = jnp.zeros((D,), jnp.float32)
    query_gain_sum = jnp.zeros((HEAD_SIZE,), jnp.float32)
    key_gain_sum = jnp.zeros((HEAD_SIZE,), jnp.float32)
    output_list = []
    delta_list = []
    for micro_index in range(micro_count):
        input_part = group_input[micro_index]
        grad_part = group_grad[micro_index]
        input_full, grad_full = (
            lax.all_gather(input_part, "col", axis=1, tiled=True),
            lax.all_gather(grad_part, "col", axis=1, tiled=True),
        )
        fwd_set = (
            lax.all_gather(query_weight, "row", axis=0, tiled=True),
            lax.all_gather(key_weight, "row", axis=0, tiled=True),
            lax.all_gather(value_weight, "row", axis=0, tiled=True),
            lax.all_gather(out_weight, "row", axis=1, tiled=True),
            lax.all_gather(gate_weight, "row", axis=0, tiled=True),
            lax.all_gather(up_weight, "row", axis=0, tiled=True),
            lax.all_gather(down_weight, "row", axis=1, tiled=True),
        )
        query_full, key_full, value_full, out_full, gate_full, up_full, down_full = fwd_set
        segment = segment_ids(seq_lengths[micro_index, 0], group_rows)
        allowed = (segment[:, None] == segment[None, :]) & (places[None, :] <= places[:, None])
        cosine, sine_table = rope_tables(positions[micro_index])
        input_float = input_full.astype(jnp.float32)
        scale_one = lax.rsqrt(jnp.mean(input_float * input_float, axis=-1, keepdims=True) + EPSILON)
        first_normed_input = (input_float * scale_one * gain_one).astype(jnp.bfloat16)
        query_proj = project(first_normed_input, query_full).reshape(group_rows, -1, HEAD_SIZE)
        projected_keys = project(first_normed_input, key_full).reshape(group_rows, -1, HEAD_SIZE)
        value_rows = (
            project(first_normed_input, value_full)
            .astype(jnp.bfloat16)
            .reshape(group_rows, -1, HEAD_SIZE)
        )
        query_inv = lax.rsqrt(jnp.mean(query_proj * query_proj, axis=-1, keepdims=True) + EPSILON)
        query_hat = query_proj * query_inv
        query_norm = query_hat * query_scale
        key_inv = lax.rsqrt(
            jnp.mean(projected_keys * projected_keys, axis=-1, keepdims=True) + EPSILON
        )
        key_hat = projected_keys * key_inv
        key_norm = key_hat * key_scale
        rotated_queries = (
            query_norm * cosine[:, None, :] + rotate(query_norm) * sine_table[:, None, :]
        ).astype(jnp.bfloat16)
        key_rows = (
            key_norm * cosine[:, None, :] + rotate(key_norm) * sine_table[:, None, :]
        ).astype(jnp.bfloat16)
        kv_heads = key_rows.shape[1]
        repeats = rotated_queries.shape[1] // kv_heads
        grouped_queries = rotated_queries.reshape(group_rows, kv_heads, repeats, HEAD_SIZE)
        scores = block_scores(grouped_queries, key_rows, allowed)
        row_top = jnp.max(scores, axis=-1, keepdims=True)
        exp_scores = jnp.exp(scores - row_top)
        row_sum = jnp.sum(exp_scores, axis=-1, keepdims=True)
        softmax = exp_scores / row_sum
        head_out = jnp.einsum(
            "krqt,tkd->qkrd",
            softmax.astype(jnp.bfloat16),
            value_rows,
            preferred_element_type=jnp.float32,
        )
        attended_list = head_out.astype(jnp.bfloat16).reshape(block_size, -1)
        lse_list = row_top + jnp.log(row_sum)
        attn_partial = project(attended_list, out_full)
        resid_full = input_float + sum_whole(attn_partial)
        scale_two = lax.rsqrt(jnp.mean(resid_full * resid_full, axis=-1, keepdims=True) + EPSILON)
        hat_full = resid_full * scale_two
        normed_two = (hat_full * gain_two).astype(jnp.bfloat16)
        resid_part = lax.dynamic_slice_in_dim(resid_full, my_start, width_part, 1)
        gate_value = project(normed_two, gate_full)
        up_value = project(normed_two, up_full)
        sigma_gate = jax.nn.sigmoid(gate_value)
        activated = gate_value * sigma_gate
        hidden = (activated * up_value).astype(jnp.bfloat16)
        output_part = resid_part + lax.psum_scatter(
            project(hidden, down_full).astype(jnp.bfloat16), "col", scatter_dimension=1, tiled=True
        ).astype(jnp.float32)
        output_rows = output_part.astype(jnp.bfloat16)
        back_set = (
            lax.all_gather(query_weight, "row", axis=0, tiled=True),
            lax.all_gather(key_weight, "row", axis=0, tiled=True),
            lax.all_gather(value_weight, "row", axis=0, tiled=True),
            lax.all_gather(out_weight, "row", axis=1, tiled=True),
            lax.all_gather(gate_weight, "row", axis=0, tiled=True),
            lax.all_gather(up_weight, "row", axis=0, tiled=True),
            lax.all_gather(down_weight, "row", axis=1, tiled=True),
        )
        query_full, key_full, value_full, out_full, gate_full, up_full, down_full = back_set
        delta_hidden = project_back(grad_full, down_full)
        down_term = weight_term(hidden, grad_full)
        delta_gate = (
            delta_hidden * up_value * sigma_gate * (1.0 + gate_value * (1.0 - sigma_gate))
        ).astype(jnp.bfloat16)
        delta_up = (delta_hidden * activated).astype(jnp.bfloat16)
        gate_term = weight_term(normed_two, delta_gate)
        up_term = weight_term(normed_two, delta_up)
        normed_two_partial = project_back(delta_gate, gate_full) + project_back(delta_up, up_full)
        delta_two = sum_whole(normed_two_partial)
        scaled = delta_two * gain_two
        mlp_gain_sum = mlp_gain_sum + jnp.sum(delta_two * hat_full, axis=0) * column_mask
        row_inner = jnp.mean(scaled * hat_full, axis=-1, keepdims=True)
        resid_whole = grad_full.astype(jnp.float32) + scale_two * (scaled - hat_full * row_inner)
        resid_rounded = resid_whole.astype(jnp.bfloat16)
        resid_delta = lax.dynamic_slice_in_dim(resid_whole, my_start, width_part, 1)
        out_term = weight_term(attended_list, resid_rounded)
        delta_attended = (
            project_back(resid_rounded, out_full)
            .astype(jnp.bfloat16)
            .reshape(group_rows, kv_heads, repeats, HEAD_SIZE)
        )
        scores = block_scores(grouped_queries, key_rows, allowed)
        softmax = jnp.exp(scores - lse_list)
        delta_probs = jnp.einsum(
            "qkrd,tkd->krqt", delta_attended, value_rows, preferred_element_type=jnp.float32
        )
        delta_value_sum = jnp.einsum(
            "krqt,qkrd->tkd",
            softmax.astype(jnp.bfloat16),
            delta_attended,
            preferred_element_type=jnp.float32,
        )
        delta_scores = (
            softmax * (delta_probs - jnp.sum(delta_probs * softmax, axis=-1, keepdims=True))
        ).astype(jnp.bfloat16)
        delta_query_list = jnp.einsum(
            "krqt,tkd->qkrd", delta_scores, key_rows, preferred_element_type=jnp.float32
        ) * (1.0 / math.sqrt(HEAD_SIZE))
        delta_key_sum = jnp.einsum(
            "krqt,qkrd->tkd", delta_scores, grouped_queries, preferred_element_type=jnp.float32
        ) * (1.0 / math.sqrt(HEAD_SIZE))
        delta_query_rot = delta_query_list.reshape(group_rows, -1, HEAD_SIZE)
        delta_query_norm = delta_query_rot * cosine[:, None, :] + unrotate(
            delta_query_rot * sine_table[:, None, :]
        )
        delta_key_norm = delta_key_sum * cosine[:, None, :] + unrotate(
            delta_key_sum * sine_table[:, None, :]
        )
        query_gain_sum = query_gain_sum + jnp.sum(delta_query_norm * query_hat, axis=(0, 1))
        key_gain_sum = key_gain_sum + jnp.sum(delta_key_norm * key_hat, axis=(0, 1))
        query_scaled = delta_query_norm * query_scale
        key_scaled = delta_key_norm * key_scale
        delta_query_proj = (
            (
                query_inv
                * (
                    query_scaled
                    - query_hat * jnp.mean(query_scaled * query_hat, axis=-1, keepdims=True)
                )
            )
            .astype(jnp.bfloat16)
            .reshape(group_rows, -1)
        )
        delta_key_proj = (
            (
                key_inv
                * (key_scaled - key_hat * jnp.mean(key_scaled * key_hat, axis=-1, keepdims=True))
            )
            .astype(jnp.bfloat16)
            .reshape(group_rows, -1)
        )
        delta_value_proj = delta_value_sum.astype(jnp.bfloat16).reshape(group_rows, -1)
        query_term = weight_term(first_normed_input, delta_query_proj)
        key_term = weight_term(first_normed_input, delta_key_proj)
        value_term = weight_term(first_normed_input, delta_value_proj)
        normed_one_partial = (
            project_back(delta_query_proj, query_full)
            + project_back(delta_key_proj, key_full)
            + project_back(delta_value_proj, value_full)
        )
        delta_one = sum_whole(normed_one_partial)
        hat_one = input_float * scale_one
        scaled = delta_one * gain_one
        attn_gain_sum = attn_gain_sum + jnp.sum(delta_one * hat_one, axis=0) * column_mask
        row_inner = jnp.mean(scaled * hat_one, axis=-1, keepdims=True)
        norm_delta = scale_one * (scaled - hat_one * row_inner)
        input_delta = resid_delta + lax.dynamic_slice_in_dim(norm_delta, my_start, width_part, 1)
        grad_terms = (
            lax.psum_scatter(
                query_term.astype(jnp.bfloat16), "row", scatter_dimension=0, tiled=True
            ).astype(jnp.float32),
            lax.psum_scatter(
                key_term.astype(jnp.bfloat16), "row", scatter_dimension=0, tiled=True
            ).astype(jnp.float32),
            lax.psum_scatter(
                value_term.astype(jnp.bfloat16), "row", scatter_dimension=0, tiled=True
            ).astype(jnp.float32),
            lax.psum_scatter(
                out_term.astype(jnp.bfloat16), "row", scatter_dimension=1, tiled=True
            ).astype(jnp.float32),
            lax.psum_scatter(
                gate_term.astype(jnp.bfloat16), "row", scatter_dimension=0, tiled=True
            ).astype(jnp.float32),
            lax.psum_scatter(
                up_term.astype(jnp.bfloat16), "row", scatter_dimension=0, tiled=True
            ).astype(jnp.float32),
            lax.psum_scatter(
                down_term.astype(jnp.bfloat16), "row", scatter_dimension=1, tiled=True
            ).astype(jnp.float32),
        )
        grad_totals = [
            left_side + right_side for left_side, right_side in zip(grad_totals, grad_terms)
        ]
        slot_rows = slots_in[micro_index]
        output_back = jnp.take(output_rows, slot_rows, axis=0).reshape(
            row_size, piece_rows, width_part
        )
        delta_back = jnp.take(input_delta.astype(jnp.bfloat16), slot_rows, axis=0).reshape(
            row_size, piece_rows, width_part
        )
        output_home, delta_home = (
            lax.all_to_all(output_back, "row", split_axis=0, concat_axis=0, tiled=True),
            lax.all_to_all(delta_back, "row", split_axis=0, concat_axis=0, tiled=True),
        )
        output_list.append(
            jnp.take(output_home.reshape(group_rows, width_part), given_rank[micro_index], axis=0)
        )
        delta_list.append(
            jnp.take(delta_home.reshape(group_rows, width_part), given_rank[micro_index], axis=0)
        )
    attn_gain_grad, mlp_gain_grad, query_gain_grad, key_gain_grad = lax.psum(
        (attn_gain_sum, mlp_gain_sum, query_gain_sum, key_gain_sum), ("row", "col")
    )
    layer_output = jnp.stack(output_list, axis=0)
    input_grad = jnp.stack(delta_list, axis=0)
    return (
        layer_output,
        input_grad,
        attn_gain_grad,
        grad_totals[0],
        grad_totals[1],
        grad_totals[2],
        query_gain_grad,
        key_gain_grad,
        grad_totals[3],
        mlp_gain_grad,
        grad_totals[4],
        grad_totals[5],
        grad_totals[6],
    )


def solution(mesh):
    in_specs = (
        P(None, "row", "col"),
        P(None, "row", "col"),
        P(None, "row"),
        P(None, "row", None),
        P(None, "row"),
        P(),
        P("row", "col"),
        P("row", "col"),
        P("row", "col"),
        P(),
        P(),
        P("col", "row"),
        P(),
        P("row", "col"),
        P("row", "col"),
        P("col", "row"),
    )
    out_specs = (
        P(None, "row", "col"),
        P(None, "row", "col"),
        P(),
        P("row", "col"),
        P("row", "col"),
        P("row", "col"),
        P(),
        P(),
        P("col", "row"),
        P(),
        P("row", "col"),
        P("row", "col"),
        P("col", "row"),
    )
    return jax.shard_map(body, mesh=mesh, in_specs=in_specs, out_specs=out_specs, check_vma=False)
```

profile of v0, /device:TPU:2, one launch (start us, length us, event | category | flops | bytes accessed | tf_op | source)
XLA Modules:
  0.0 1760.3 jit_solution(6509874647805770056)
XLA Ops:
  203.1 26.5 %all_gather.27 = bf16[1024,384]{1,0:T(8,128)(2,1)S(1)} all-gather(bf16[64,384]{1,0:T(8,128)(2,1)S(1)} %copy-done.115), channel_id=1, replica_groups=mesh['row'=16,'col'=8] {'row'}, dimensions={0}, use_global_device_ids=true | all-gather | bytes 835584 | tf_op jit(solution)/shard_map/all_gather | solution.py:155
  229.6 24.4 %all_gather.28 = bf16[1024,384]{1,0:T(8,128)(2,1)} all-gather(bf16[64,384]{1,0:T(8,128)(2,1)S(1)} %copy-done.116), channel_id=1, replica_groups=mesh['row'=16,'col'=8] {'row'}, dimensions={0}, use_global_device_ids=true | all-gather | bytes 835584 | tf_op jit(solution)/shard_map/all_gather | solution.py:156
  254.0 27.1 %all_gather.29 = bf16[384,1024]{0,1:T(8,128)(2,1)} all-gather(bf16[384,64]{0,1:T(8,128)(2,1)S(1)} %copy-done.117), channel_id=1, replica_groups=mesh['row'=16,'col'=8] {'row'}, dimensions={1}, use_global_device_ids=true | all-gather | bytes 835584 | tf_op jit(solution)/shard_map/all_gather | solution.py:157
  281.4 27.3 %all-reduce.12.cloned.1.call-done = (f32[512,1024]{1,0:T(8,128)}, f32[512,1024]{1,0:T(8,128)}) async-done(((f32[512,1024]{1,0:T(8,128)}, f32[512,1024]{1,0:T(8,128)}), (f32[512,1024]{1,0:T(8,128)}, f32[512,1024]{1,0:T(8,128)})) %all-reduce.12.cloned.1.call-update) | async-done | bytes 4194320 | tf_op jit(solution)/shard_map/psum | solution.py:70
  320.3 28.0 %all-gather.15.cloned.1.call-done = bf16[1,512,1024]{2,1,0:T(8,128)(2,1)} async-done(((bf16[1,512,128]{2,1,0:T(8,128)(2,1)}), bf16[1,512,1024]{2,1,0:T(8,128)(2,1)}) %all-gather.15.cloned.1.call-update) | async-done | bytes 1048592 | tf_op jit(solution)/shard_map/all_gather | solution.py:148
  354.9 47.2 %all-gather.13.cloned.1.call-done = bf16[1,512,1024]{2,1,0:T(8,128)(2,1)} async-done(((bf16[1,512,128]{2,1,0:T(8,128)(2,1)}), bf16[1,512,1024]{2,1,0:T(8,128)(2,1)}) %all-gather.13.cloned.1.call-update) | async-done | bytes 1048592 | tf_op jit(solution)/shard_map/all_gather | solution.py:148
  444.2 73.8 %all-reduce.10.cloned.1.call-done = (f32[512,1024]{1,0:T(8,128)}, f32[512,1024]{1,0:T(8,128)}) async-done(((f32[512,1024]{1,0:T(8,128)}, f32[512,1024]{1,0:T(8,128)}), (f32[512,1024]{1,0:T(8,128)}, f32[512,1024]{1,0:T(8,128)})) %all-reduce.10.cloned.1.call-update) | async-done | bytes 4194320 | tf_op jit(solution)/shard_map/psum | solution.py:70
  595.7 69.5 %reduce-scatter.47.cloned.1.call-done = bf16[384,64]{0,1:T(8,128)(2,1)} async-done(((bf16[384,1024]{0,1:T(8,128)(2,1)}), bf16[384,64]{0,1:T(8,128)(2,1)}) %reduce-scatter.47.cloned.1.call-update) | async-done | bytes 49168 | tf_op jit(solution)/shard_map/reduce_scatter | solution.py:335
  666.6 67.3 %reduce-scatter.37.cloned.1.call-done = bf16[64,384]{1,0:T(8,128)(2,1)} async-done(((bf16[1024,384]{1,0:T(8,128)(2,1)}), bf16[64,384]{1,0:T(8,128)(2,1)}) %reduce-scatter.37.cloned.1.call-update) | async-done | bytes 49168 | tf_op jit(solution)/shard_map/reduce_scatter | solution.py:329
  733.9 69.4 %reduce-scatter.39.cloned.1.call-done = bf16[64,384]{1,0:T(8,128)(2,1)} async-done(((bf16[1024,384]{1,0:T(8,128)(2,1)}), bf16[64,384]{1,0:T(8,128)(2,1)}) %reduce-scatter.39.cloned.1.call-update) | async-done | bytes 49168 | tf_op jit(solution)/shard_map/reduce_scatter | solution.py:329
  804.8 67.3 %reduce-scatter.41.cloned.1.call-done = bf16[64,384]{1,0:T(8,128)(2,1)} async-done(((bf16[1024,384]{1,0:T(8,128)(2,1)}), bf16[64,384]{1,0:T(8,128)(2,1)}) %reduce-scatter.41.cloned.1.call-update) | async-done | bytes 49168 | tf_op jit(solution)/shard_map/reduce_scatter | solution.py:332
  872.2 69.3 %reduce-scatter.43.cloned.1.call-done = bf16[64,384]{1,0:T(8,128)(2,1)} async-done(((bf16[1024,384]{1,0:T(8,128)(2,1)}), bf16[64,384]{1,0:T(8,128)(2,1)}) %reduce-scatter.43.cloned.1.call-update) | async-done | bytes 49168 | tf_op jit(solution)/shard_map/reduce_scatter | solution.py:332
  942.9 36.2 %reduce-scatter.49.cloned.1.call-done = bf16[128,512]{1,0:T(8,128)(2,1)} async-done(((bf16[1024,512]{1,0:T(8,128)(2,1)}), bf16[128,512]{1,0:T(8,128)(2,1)}) %reduce-scatter.49.cloned.1.call-update) | async-done | bytes 131088
  984.0 35.3 %reduce-scatter.51.cloned.1.call-done = bf16[128,512]{1,0:T(8,128)(2,1)} async-done(((bf16[1024,512]{1,0:T(8,128)(2,1)}), bf16[128,512]{1,0:T(8,128)(2,1)}) %reduce-scatter.51.cloned.1.call-update) | async-done | bytes 131088
  1025.9 63.6 %reduce-scatter.29.cloned.1.call-done = bf16[64,128]{1,0:T(8,128)(2,1)} async-done(((bf16[1024,128]{1,0:T(8,128)(2,1)}), bf16[64,128]{1,0:T(8,128)(2,1)}) %reduce-scatter.29.cloned.1.call-update) | async-done | bytes 16400 | tf_op jit(solution)/shard_map/reduce_scatter | solution.py:323
  1089.4 67.9 %reduce-scatter.31.cloned.1.call-done = bf16[64,128]{1,0:T(8,128)(2,1)} async-done(((bf16[1024,128]{1,0:T(8,128)(2,1)}), bf16[64,128]{1,0:T(8,128)(2,1)}) %reduce-scatter.31.cloned.1.call-update) | async-done | bytes 16400 | tf_op jit(solution)/shard_map/reduce_scatter | solution.py:323
  1158.6 66.3 %reduce-scatter.27.cloned.1.call-done = bf16[64,128]{1,0:T(8,128)(2,1)} async-done(((bf16[1024,128]{1,0:T(8,128)(2,1)}), bf16[64,128]{1,0:T(8,128)(2,1)}) %reduce-scatter.27.cloned.1.call-update) | async-done | bytes 16400 | tf_op jit(solution)/shard_map/reduce_scatter | solution.py:320
  1225.0 67.9 %reduce-scatter.25.cloned.1.call-done = bf16[64,128]{1,0:T(8,128)(2,1)} async-done(((bf16[1024,128]{1,0:T(8,128)(2,1)}), bf16[64,128]{1,0:T(8,128)(2,1)}) %reduce-scatter.25.cloned.1.call-update) | async-done | bytes 16400 | tf_op jit(solution)/shard_map/reduce_scatter | solution.py:320
  1294.2 67.0 %reduce-scatter.35.cloned.1.call-done = bf16[256,64]{0,1:T(8,128)(2,1)} async-done(((bf16[256,1024]{0,1:T(8,128)(2,1)}), bf16[256,64]{0,1:T(8,128)(2,1)}) %reduce-scatter.35.cloned.1.call-update) | async-done | bytes 32784 | tf_op jit(solution)/shard_map/reduce_scatter | solution.py:326
  1361.2 68.7 %reduce-scatter.33.cloned.1.call-done = bf16[256,64]{0,1:T(8,128)(2,1)} async-done(((bf16[256,1024]{0,1:T(8,128)(2,1)}), bf16[256,64]{0,1:T(8,128)(2,1)}) %reduce-scatter.33.cloned.1.call-update) | async-done | bytes 32784 | tf_op jit(solution)/shard_map/reduce_scatter | solution.py:326
  1431.3 103.6 %all-reduce.8.cloned.1.call-done = (f32[512,1024]{1,0:T(8,128)}, f32[512,1024]{1,0:T(8,128)}) async-done(((f32[512,1024]{1,0:T(8,128)}, f32[512,1024]{1,0:T(8,128)}), (f32[512,1024]{1,0:T(8,128)}, f32[512,1024]{1,0:T(8,128)})) %all-reduce.8.cloned.1.call-update) | async-done | bytes 4194320 | tf_op jit(solution)/shard_map/psum | solution.py:70
  1573.7 31.5 %reduce-scatter.21.cloned.1.call-done = bf16[64,256]{1,0:T(8,128)(2,1)} async-done(((bf16[1024,256]{1,0:T(8,128)(2,1)}), bf16[64,256]{1,0:T(8,128)(2,1)}) %reduce-scatter.21.cloned.1.call-update) | async-done | bytes 32784 | tf_op jit(solution)/shard_map/reduce_scatter | solution.py:317
  1605.2 68.6 %reduce-scatter.23.cloned.1.call-done = bf16[64,256]{1,0:T(8,128)(2,1)} async-done(((bf16[1024,256]{1,0:T(8,128)(2,1)}), bf16[64,256]{1,0:T(8,128)(2,1)}) %reduce-scatter.23.cloned.1.call-update) | async-done | bytes 32784 | tf_op jit(solution)/shard_map/reduce_scatter | solution.py:317
  1680.0 66.4 %all-reduce = (f32[1024]{0:T(1024)}, f32[128]{0:T(128)}, f32[128]{0:T(128)}, f32[1024]{0:T(1024)}) all-reduce(f32[1024]{0:T(1024)S(1)} %select_add_fusion.1, f32[128]{0:T(128)S(1)} %add.347, f32[128]{0:T(128)S(1)} %add.348, f32[1024]{0:T(1024)S(1)} %select_add_fusion), channel_id=1, replica_groups=mesh['row'=16,'col'=8] {'row','col'}, use_global_device_ids=true, to_apply=%region_39.42 | all-reduce | flops 2304 | bytes 18432 | tf_op jit(solution)/shard_map/psum | solution.py:359
  (603 shorter events, 403.7 us)
Async XLA Ops:
  66.6 111.3 %all-gather.11.cloned.1.call-start = ((), (), s32[]{:S(2)}) async-start(), calls=%async_computation.38 | async-start | bytes 1179648 | tf_op jit(solution)/shard_map/all_gather | solution.py:147
  83.7 95.9 %all-gather.9.cloned.1.call-start = ((), (), s32[]{:S(2)}) async-start(), calls=%async_computation.37 | async-start | bytes 1179648 | tf_op jit(solution)/shard_map/all_gather | solution.py:147
  128.6 180.1 %all-reduce.12.cloned.1.call-start = ((), (), s32[]{:S(2)}) async-start(), calls=%async_computation.45 | async-start | bytes 8388608 | tf_op jit(solution)/shard_map/psum | solution.py:70
  200.8 147.5 %all-gather.15.cloned.1.call-start = ((), (), s32[]{:S(2)}) async-start(), calls=%async_computation.40 | async-start | bytes 1179648 | tf_op jit(solution)/shard_map/all_gather | solution.py:148
  202.5 199.6 %all-gather.13.cloned.1.call-start = ((), (), s32[]{:S(2)}) async-start(), calls=%async_computation.39 | async-start | bytes 1179648 | tf_op jit(solution)/shard_map/all_gather | solution.py:148
  281.2 236.8 %all-reduce.10.cloned.1.call-start = ((), (), s32[]{:S(2)}) async-start(), calls=%async_computation.44 | async-start | bytes 8388608 | tf_op jit(solution)/shard_map/psum | solution.py:70
  412.7 183.0 %reduce-scatter.45.cloned.1.call-start = ((), (), s32[]{:S(2)}) async-start(), calls=%async_computation.35 | async-start | bytes 835584 | tf_op jit(solution)/shard_map/reduce_scatter | solution.py:335
  415.8 249.3 %reduce-scatter.47.cloned.1.call-start = ((), (), s32[]{:S(2)}) async-start(), calls=%async_computation.36 | async-start | bytes 835584 | tf_op jit(solution)/shard_map/reduce_scatter | solution.py:335
  418.9 315.1 %reduce-scatter.37.cloned.1.call-start = ((), (), s32[]{:S(2)}) async-start(), calls=%async_computation.31 | async-start | bytes 835584 | tf_op jit(solution)/shard_map/reduce_scatter | solution.py:329
  421.9 381.4 %reduce-scatter.39.cloned.1.call-start = ((), (), s32[]{:S(2)}) async-start(), calls=%async_computation.32 | async-start | bytes 835584 | tf_op jit(solution)/shard_map/reduce_scatter | solution.py:329
  424.9 447.2 %reduce-scatter.41.cloned.1.call-start = ((), (), s32[]{:S(2)}) async-start(), calls=%async_computation.33 | async-start | bytes 835584 | tf_op jit(solution)/shard_map/reduce_scatter | solution.py:332
  427.9 513.6 %reduce-scatter.43.cloned.1.call-start = ((), (), s32[]{:S(2)}) async-start(), calls=%async_computation.34 | async-start | bytes 835584 | tf_op jit(solution)/shard_map/reduce_scatter | solution.py:332
  430.9 548.1 %reduce-scatter.49.cloned.1.call-start = ((), (), s32[]{:S(2)}) async-start(), calls=%async_computation.41 | async-start | bytes 1179648
  436.0 583.2 %reduce-scatter.51.cloned.1.call-start = ((), (), s32[]{:S(2)}) async-start(), calls=%async_computation.42 | async-start | bytes 1179648
  444.1 645.3 %reduce-scatter.29.cloned.1.call-start = ((), (), s32[]{:S(2)}) async-start(), calls=%async_computation.27 | async-start | bytes 278528 | tf_op jit(solution)/shard_map/reduce_scatter | solution.py:323
  548.6 608.7 %reduce-scatter.31.cloned.1.call-start = ((), (), s32[]{:S(2)}) async-start(), calls=%async_computation.28 | async-start | bytes 278528 | tf_op jit(solution)/shard_map/reduce_scatter | solution.py:323
  555.0 670.0 %reduce-scatter.27.cloned.1.call-start = ((), (), s32[]{:S(2)}) async-start(), calls=%async_computation.26 | async-start | bytes 278528 | tf_op jit(solution)/shard_map/reduce_scatter | solution.py:320
  561.4 731.5 %reduce-scatter.25.cloned.1.call-start = ((), (), s32[]{:S(2)}) async-start(), calls=%async_computation.25 | async-start | bytes 278528 | tf_op jit(solution)/shard_map/reduce_scatter | solution.py:320
  568.8 792.4 %reduce-scatter.35.cloned.1.call-start = ((), (), s32[]{:S(2)}) async-start(), calls=%async_computation.30 | async-start | bytes 557056 | tf_op jit(solution)/shard_map/reduce_scatter | solution.py:326
  574.5 855.4 %reduce-scatter.33.cloned.1.call-start = ((), (), s32[]{:S(2)}) async-start(), calls=%async_computation.29 | async-start | bytes 557056 | tf_op jit(solution)/shard_map/reduce_scatter | solution.py:326
  580.2 954.7 %all-reduce.8.cloned.1.call-start = ((), (), s32[]{:S(2)}) async-start(), calls=%async_computation.43 | async-start | bytes 8388608 | tf_op jit(solution)/shard_map/psum | solution.py:70
  588.1 1017.1 %reduce-scatter.21.cloned.1.call-start = ((), (), s32[]{:S(2)}) async-start(), calls=%async_computation.23 | async-start | bytes 557056 | tf_op jit(solution)/shard_map/reduce_scatter | solution.py:317
  982.9 690.9 %reduce-scatter.23.cloned.1.call-start = ((), (), s32[]{:S(2)}) async-start(), calls=%async_computation.24 | async-start | bytes 557056 | tf_op jit(solution)/shard_map/reduce_scatter | solution.py:317
  1570.2 105.0 %all-to-all-start.3 = ((bf16[16,32,128]{2,1,0:T(8,128)(2,1)}), bf16[16,32,128]{2,1,0:T(8,128)(2,1)S(1)}, u32[]{:S(2)}, u32[]{:S(2)}) async-start(bf16[16,32,128]{2,1,0:T(8,128)(2,1)} %bitcast.55), calls=%async_computation.3 | async-start | bytes 262144 | tf_op jit(solution)/shard_map/all_to_all | solution.py:350
  (174 other events, 4194.7 us)
Sparse Core Ops, SparseCore 0:
  83.8 35.9 all-gather.10
  128.7 38.1 all-gather.8
  200.9 107.7 all-reduce.11
  310.7 37.5 all-gather.14
  350.4 51.5 all-gather.12
  412.1 105.8 all-reduce.9
  521.0 3.6 sort.51.cloned.1.call-done
  528.6 67.0 reduce-scatter.44
  600.0 65.1 reduce-scatter.46
  668.8 65.0 reduce-scatter.36
  738.2 65.0 reduce-scatter.38
  807.0 65.1 reduce-scatter.40
  876.3 65.0 reduce-scatter.42
  943.7 35.3 reduce-scatter.48
  981.3 37.8 reduce-scatter.50
  1022.8 66.6 reduce-scatter.28
  1093.1 64.1 reduce-scatter.30
  1160.8 64.1 reduce-scatter.26
  1228.7 64.1 reduce-scatter.24
  1296.5 64.6 reduce-scatter.34
  1365.4 64.5 reduce-scatter.32
  1432.3 102.5 all-reduce.7
  1538.6 66.5 reduce-scatter.20
  1609.2 64.5 reduce-scatter.22
  (5 shorter events, 6.3 us)
where the time goes:
time: 1770 us; the launch traced here: 1760 us
  waiting for transfers between devices  1220 us (69%)
  blocking collectives  234 us (13%)
  matrix products  96.7 us (5%)
  local copies, waits for them, and re-layouts  80.4 us (5%)
  other arithmetic  67.7 us (4%)
  starting transfers between devices  39.5 us (2%)
    psum x3, waiting for transfers between devices, sum_whole(): return lax.psum(partial_value, 'col')  205 us
    reduce_scatter x2, waiting for transfers between devices, body(): lax.psum_scatter(gate_term.astype(jnp.bfloat16), 'row', scatter_dimension...  137 us
    reduce_scatter x2, waiting for transfers between devices, body(): lax.psum_scatter(up_term.astype(jnp.bfloat16), 'row', scatter_dimension=0...  137 us
    reduce_scatter x2, waiting for transfers between devices, body(): lax.psum_scatter(out_term.astype(jnp.bfloat16), 'row', scatter_dimension=...  136 us
    reduce_scatter x2, waiting for transfers between devices, body(): lax.psum_scatter(key_term.astype(jnp.bfloat16), 'row', scatter_dimension=...  134 us
    reduce_scatter x2, waiting for transfers between devices, body(): lax.psum_scatter(value_term.astype(jnp.bfloat16), 'row', scatter_dimensio...  131 us
    reduce_scatter x2, waiting for transfers between devices, body(): lax.psum_scatter(query_term.astype(jnp.bfloat16), 'row', scatter_dimensio...  100 us
    reduce_scatter x2, waiting for transfers between devices, body(): lax.psum_scatter(down_term.astype(jnp.bfloat16), 'row', scatter_dimension...  75.8 us
  transfers between devices with their start and end apart: 30, of which 25 were waited for; matrix products, arithmetic and copies ran while one was open for 10% of the time, Pallas kernels for 0%

commit v1 on v0

v1 whole, which is shorter than its diff:
```python
import math

import jax
import jax.numpy as jnp
from jax import lax
from jax.sharding import PartitionSpec as P

D = 1024
HEAD_SIZE = 128
EPSILON = 1e-06
ROPE_BASE = 1000000.0
NEGATIVE = -1e30
BOTH = ("row", "col")
ROWS = 16
BF = jnp.bfloat16
F32 = jnp.float32


def flat(row, col):
    return row * 8 + col


SAME_X = [[0, 1, 2, 3], [4, 5, 6, 7]]
CORES = [[2 * k, 2 * k + 1] for k in range(8)]
PLANE = [
    [flat(2 * k + core, 4 * y_lo + x) for k in range(8) for y_lo in range(2)]
    for x in range(4)
    for core in range(2)
]


def dot(a, b, dims):
    return lax.dot_general(a, b, (dims, ((), ())), preferred_element_type=F32)


def nn(a, b):
    return dot(a, b, ((1,), (0,)))


def nt(a, b):
    return dot(a, b, ((1,), (1,)))


def tn(a, b):
    return dot(a, b, ((0,), (0,)))


def exchange(blocks, axis, groups=None):
    return lax.all_to_all(blocks, axis, 0, 0, axis_index_groups=groups, tiled=True)


def rotate(t):
    half = t.shape[-1] // 2
    return jnp.concatenate([-t[..., half:], t[..., :half]], axis=-1)


def unrotate(t):
    half = t.shape[-1] // 2
    return jnp.concatenate([t[..., half:], -t[..., :half]], axis=-1)


def collect_weight(shard):
    n = shard.shape[1]
    plane = exchange(jnp.broadcast_to(shard[None], (16, 64, n)), BOTH, PLANE)
    pair = exchange(jnp.broadcast_to(plane[None], (2, 16, 64, n)), "row", CORES)
    pair = pair.reshape(2, 8, 2, 64, n)
    return jnp.transpose(pair, (1, 0, 3, 2, 4)).reshape(1024, 2, n)


def reduce_weight(grad):
    n = grad.shape[2]
    parts = jnp.transpose(grad.reshape(8, 2, 64, 2, n), (1, 0, 3, 2, 4)).astype(BF)
    parts = exchange(parts, "row", CORES)
    half = (parts[0].astype(F32) + parts[1].astype(F32)).astype(BF)
    got = exchange(half.reshape(16, 64, n), BOTH, PLANE)
    return jnp.sum(got.astype(F32), axis=0)


def send_tokens(rows):
    parts = jnp.transpose(rows.reshape(2, ROWS, 32, 128), (1, 0, 2, 3))
    parts = jnp.broadcast_to(parts[:, :, None], (ROWS, 2, 4, 32, 128)).reshape(128, 32, 128)
    got = exchange(parts, BOTH).reshape(ROWS, 8, 32, 128)
    return jnp.transpose(got, (0, 2, 1, 3)).reshape(512, 1024)


def return_tokens(part):
    parts = jnp.transpose(part.astype(BF).reshape(ROWS, 32, 8, 128), (0, 2, 1, 3))
    got = exchange(parts.reshape(128, 32, 128), BOTH).reshape(ROWS, 2, 4, 32, 128)
    total = jnp.sum(got.astype(F32), axis=2)
    return jnp.transpose(total, (1, 0, 2, 3)).reshape(2, 512, 128)


def scatter_sum(part):
    parts = jnp.transpose(part.astype(BF).reshape(512, 2, 4, 128), (2, 0, 1, 3))
    got = exchange(parts, "col", SAME_X)
    return jnp.sum(got.astype(F32), axis=0)


def collect_features(mine):
    got = exchange(jnp.broadcast_to(mine[None], (4, 512, 2, 128)), "col", SAME_X)
    return jnp.transpose(got, (1, 2, 0, 3)).reshape(512, 1024)


def body(
    layer_input,
    out_grad,
    token_route,
    seq_lengths,
    positions,
    attn_gain,
    query_weight,
    key_weight,
    value_weight,
    query_gain,
    key_gain,
    out_weight,
    mlp_gain,
    gate_weight,
    up_weight,
    down_weight,
):
    col = lax.axis_index("col")
    y_lo = col // 4
    x = col % 4
    places = jnp.arange(512, dtype=jnp.int32)

    rank = jnp.sum((token_route[:, None, :] < token_route[:, :, None]).astype(jnp.int32), axis=2)
    chosen = places[None, :, None] == rank[:, None, :]
    pick = chosen.astype(BF)
    slots_out = jnp.sum(jnp.where(chosen, (token_route % 512)[:, None, :], 0), axis=2)
    slots_all = exchange(jnp.transpose(slots_out.reshape(2, ROWS, 32), (1, 0, 2)), "row")
    slots = lax.dynamic_index_in_dim(slots_all, y_lo, 1, keepdims=False).reshape(512)

    def sort_rows(table):
        return jnp.stack([nn(pick[m], table[m]).astype(BF) for m in range(2)])

    def unsort_rows(table):
        return jnp.stack([tn(pick[m], table[m].astype(BF)).astype(BF) for m in range(2)])

    inputs = send_tokens(sort_rows(layer_input))
    grads = send_tokens(sort_rows(out_grad))

    qkv_full = collect_weight(jnp.concatenate([query_weight, key_weight, value_weight], axis=1))
    rest_full = collect_weight(
        jnp.concatenate([out_weight.T, gate_weight, up_weight, down_weight.T], axis=1)
    )
    wq, wk, wv = qkv_full[:, :, :256], qkv_full[:, :, 256:384], qkv_full[:, :, 384:]
    wq, wk, wv = wq.reshape(1024, 512), wk.reshape(1024, 256), wv.reshape(1024, 256)
    wo, wg, wu, wd = (
        rest_full[:, :, :256].reshape(1024, 512),
        rest_full[:, :, 256:640].reshape(1024, 768),
        rest_full[:, :, 640:1024].reshape(1024, 768),
        rest_full[:, :, 1024:].reshape(1024, 768),
    )
    gain_one = attn_gain.astype(F32)
    gain_two = mlp_gain.astype(F32)
    query_scale = query_gain.astype(F32)
    key_scale = key_gain.astype(F32)

    lengths = lax.dynamic_index_in_dim(seq_lengths, y_lo, 0, keepdims=False)[0]
    bound_one = lengths[0]
    bound_two = bound_one + lengths[1]
    bound_three = bound_two + lengths[2]
    segment = (
        (slots >= bound_one).astype(jnp.int32)
        + (slots >= bound_two).astype(jnp.int32)
        + (slots >= bound_three).astype(jnp.int32)
    )
    allowed = (segment[:, None] == segment[None, :]) & (slots[None, :] <= slots[:, None])
    my_positions = lax.dynamic_index_in_dim(positions, y_lo, 0, keepdims=False)
    position = jnp.sum(
        jnp.where(slots[:, None] == places[None, :], my_positions[None, :], 0), axis=1
    )
    freq_steps = jnp.arange(0, HEAD_SIZE, 2).astype(F32) / HEAD_SIZE
    frequency = 1.0 / ROPE_BASE**freq_steps
    angles = position.astype(F32)[:, None] * frequency[None, :]
    angles = jnp.concatenate([angles, angles], axis=-1)
    cosine, sine = jnp.cos(angles)[:, None, :], jnp.sin(angles)[:, None, :]

    input_float = inputs.astype(F32)
    scale_one = lax.rsqrt(jnp.mean(input_float * input_float, axis=-1, keepdims=True) + EPSILON)
    hat_one = input_float * scale_one
    normed_one = (hat_one * gain_one).astype(BF)
    query_proj = nn(normed_one, wq).reshape(512, 4, HEAD_SIZE)
    key_proj = nn(normed_one, wk).reshape(512, 2, HEAD_SIZE)
    value_rows = nn(normed_one, wv).astype(BF).reshape(512, 2, HEAD_SIZE)
    query_inv = lax.rsqrt(jnp.mean(query_proj * query_proj, axis=-1, keepdims=True) + EPSILON)
    query_hat = query_proj * query_inv
    query_norm = query_hat * query_scale
    key_inv = lax.rsqrt(jnp.mean(key_proj * key_proj, axis=-1, keepdims=True) + EPSILON)
    key_hat = key_proj * key_inv
    key_norm = key_hat * key_scale
    query_rows = (query_norm * cosine + rotate(query_norm) * sine).astype(BF)
    key_rows = (key_norm * cosine + rotate(key_norm) * sine).astype(BF)
    grouped = query_rows.reshape(512, 2, 2, HEAD_SIZE)
    scores = jnp.einsum("qkrd,tkd->krqt", grouped, key_rows, preferred_element_type=F32)
    scores = jnp.where(allowed[None, None], scores * (1.0 / math.sqrt(HEAD_SIZE)), NEGATIVE)
    row_top = jnp.max(scores, axis=-1, keepdims=True)
    exp_scores = jnp.exp(scores - row_top)
    softmax = exp_scores / jnp.sum(exp_scores, axis=-1, keepdims=True)
    softmax_low = softmax.astype(BF)
    attended = jnp.einsum("krqt,tkd->qkrd", softmax_low, value_rows, preferred_element_type=F32)
    attended = attended.astype(BF).reshape(512, 512)
    summed = scatter_sum(nt(attended, wo))
    my_input = lax.dynamic_index_in_dim(inputs.reshape(512, 2, 4, 128), x, 2, keepdims=False)
    resid_mine = my_input.astype(F32) + summed
    resid = collect_features(resid_mine.astype(BF)).astype(F32)

    scale_two = lax.rsqrt(jnp.mean(resid * resid, axis=-1, keepdims=True) + EPSILON)
    hat_two = resid * scale_two
    normed_two = (hat_two * gain_two).astype(BF)
    gate = nn(normed_two, wg)
    up = nn(normed_two, wu)
    sigma = jax.nn.sigmoid(gate)
    activated = gate * sigma
    hidden = (activated * up).astype(BF)
    mine_mask = ((jnp.arange(8, dtype=jnp.int32) % 4) == x).astype(F32)[None, :, None]

    def place(mine):
        wide = jnp.broadcast_to(mine[:, :, None, :], (512, 2, 4, 128)).reshape(512, 8, 128)
        return (wide * mine_mask).reshape(512, 1024)

    output_home = return_tokens(nt(hidden, wd) + place(resid_mine))

    delta_hidden = nn(grads, wd)
    delta_gate = (delta_hidden * up * sigma * (1.0 + gate * (1.0 - sigma))).astype(BF)
    delta_up = (delta_hidden * activated).astype(BF)
    delta_two = nt(delta_gate, wg) + nt(delta_up, wu)
    mlp_gain_sum = jnp.sum(delta_two * hat_two, axis=0)
    scaled = delta_two * gain_two
    inner = jnp.mean(scaled * hat_two, axis=-1, keepdims=True)
    my_grad = lax.dynamic_index_in_dim(grads.reshape(512, 2, 4, 128), x, 2, keepdims=False)
    resid_delta = my_grad.astype(F32) + scatter_sum(scale_two * (scaled - hat_two * inner))
    resid_low = collect_features(resid_delta.astype(BF))

    delta_attended = nn(resid_low, wo).astype(BF).reshape(512, 2, 2, HEAD_SIZE)
    rest_grad = jnp.concatenate(
        [
            tn(resid_low, attended).reshape(1024, 2, 256),
            tn(normed_two, delta_gate).reshape(1024, 2, 384),
            tn(normed_two, delta_up).reshape(1024, 2, 384),
            tn(grads, hidden).reshape(1024, 2, 384),
        ],
        axis=2,
    )
    rest_total = reduce_weight(rest_grad)
    delta_probs = jnp.einsum(
        "qkrd,tkd->krqt", delta_attended, value_rows, preferred_element_type=F32
    )
    delta_value = jnp.einsum(
        "krqt,qkrd->tkd", softmax_low, delta_attended, preferred_element_type=F32
    )
    delta_scores = (
        softmax * (delta_probs - jnp.sum(delta_probs * softmax, axis=-1, keepdims=True))
    ).astype(BF)
    delta_query = jnp.einsum(
        "krqt,tkd->qkrd", delta_scores, key_rows, preferred_element_type=F32
    ) * (1.0 / math.sqrt(HEAD_SIZE))
    delta_key = jnp.einsum(
        "krqt,qkrd->tkd", delta_scores, grouped, preferred_element_type=F32
    ) * (1.0 / math.sqrt(HEAD_SIZE))
    delta_query = delta_query.reshape(512, 4, HEAD_SIZE)
    delta_query_norm = delta_query * cosine + unrotate(delta_query * sine)
    delta_key_norm = delta_key * cosine + unrotate(delta_key * sine)
    query_gain_sum = jnp.sum(delta_query_norm * query_hat, axis=(0, 1))
    key_gain_sum = jnp.sum(delta_key_norm * key_hat, axis=(0, 1))

    def norm_back(delta, hat, inv, gain):
        part = delta * gain
        part = inv * (part - hat * jnp.mean(part * hat, axis=-1, keepdims=True))
        return part.astype(BF).reshape(512, -1)

    delta_query_proj = norm_back(delta_query_norm, query_hat, query_inv, query_scale)
    delta_key_proj = norm_back(delta_key_norm, key_hat, key_inv, key_scale)
    delta_value_proj = delta_value.astype(BF).reshape(512, -1)
    delta_one = nt(delta_query_proj, wq) + nt(delta_key_proj, wk) + nt(delta_value_proj, wv)
    attn_gain_sum = jnp.sum(delta_one * hat_one, axis=0)
    scaled = delta_one * gain_one
    inner = jnp.mean(scaled * hat_one, axis=-1, keepdims=True)
    delta_home = return_tokens(scale_one * (scaled - hat_one * inner) + place(resid_delta))
    qkv_grad = jnp.concatenate(
        [
            tn(normed_one, delta_query_proj).reshape(1024, 2, 256),
            tn(normed_one, delta_key_proj).reshape(1024, 2, 128),
            tn(normed_one, delta_value_proj).reshape(1024, 2, 128),
        ],
        axis=2,
    )
    qkv_total = reduce_weight(qkv_grad)

    attn_gain_grad, mlp_gain_grad, query_gain_grad, key_gain_grad = lax.psum(
        (attn_gain_sum, mlp_gain_sum, query_gain_sum, key_gain_sum), BOTH
    )
    return (
        unsort_rows(output_home),
        unsort_rows(delta_home),
        attn_gain_grad,
        qkv_total[:, :256],
        qkv_total[:, 256:384],
        qkv_total[:, 384:],
        query_gain_grad,
        key_gain_grad,
        rest_total[:, :256].T,
        mlp_gain_grad,
        rest_total[:, 256:640],
        rest_total[:, 640:1024],
        rest_total[:, 1024:].T,
    )


def solution(mesh):
    in_specs = (
        P(None, "row", "col"),
        P(None, "row", "col"),
        P(None, "row"),
        P(None, "row", None),
        P(None, "row"),
        P(),
        P("row", "col"),
        P("row", "col"),
        P("row", "col"),
        P(),
        P(),
        P("col", "row"),
        P(),
        P("row", "col"),
        P("row", "col"),
        P("col", "row"),
    )
    out_specs = (
        P(None, "row", "col"),
        P(None, "row", "col"),
        P(),
        P("row", "col"),
        P("row", "col"),
        P("row", "col"),
        P(),
        P(),
        P("col", "row"),
        P(),
        P("row", "col"),
        P("row", "col"),
        P("col", "row"),
    )
    return jax.shard_map(body, mesh=mesh, in_specs=in_specs, out_specs=out_specs, check_vma=False)
```

time: 1770 us -> 556 us (0.31)
  waiting for transfers between devices: 1220 us -> 88.2 us
  blocking collectives: 234 us -> 124 us
  local copies, waits for them, and re-layouts: 80.4 us -> 134 us
  starting transfers between devices: 39.5 us -> 81.5 us
  matrix products: 96.7 us -> 68.2 us
  other arithmetic: 67.7 us -> 45.3 us
    reduce_scatter x14 -> x0, waiting for transfers between devices: 851 us -> none  [the longest x2 137 us: body(): lax.psum_scatter(gate_term.astype(jnp.bfloat16), 'row', scatter_dimension...]
    psum x3 -> x0, waiting for transfers between devices: 205 us -> none  [sum_whole(): return lax.psum(partial_value, 'col')]
    all_gather x7 -> x0, blocking collectives: 168 us -> none  [the longest x1 27.1 us: body(): lax.all_gather(down_weight, 'row', axis=1, tiled=True)]
    all_gather x4 -> x0, waiting for transfers between devices: 75.2 us -> none  [the longest x2 75.2 us: body(): lax.all_gather(grad_part, 'col', axis=1, tiled=True)]
    unnamed x25 -> x0, waiting for transfers between devices: 71.8 us -> none
    all_to_all x7 -> x14, waiting for transfers between devices: 22.5 us -> 88.2 us  [exchange(): lax.all_to_all(blocks, axis, 0, 0, axis_index_groups=groups, tiled=True)]
    all_to_all x7 -> x14, starting transfers between devices: 37.7 us -> 81.5 us  [exchange(): lax.all_to_all(blocks, axis, 0, 0, axis_index_groups=groups, tiled=True)]
    gather x14 -> x0, local copies, waits for them, and re-layouts: 43.1 us -> none  [the longest x6 32.4 us: pick_rows(): jnp.take(rows_in, rows_at, axis=0)]
  transfers between devices with their start and end apart: 30 -> 14, of which waited for: 25 -> 8; matrix products, arithmetic and copies ran while one was open for 10% -> 28% of each run, Pallas kernels for 0% -> 0%
where the time goes in v1:
time: 556 us; the launch traced here: 545 us
  local copies, waits for them, and re-layouts  134 us (24%)
  blocking collectives  124 us (22%)
  waiting for transfers between devices  88.2 us (16%)
  starting transfers between devices  81.5 us (15%)
  matrix products  68.2 us (12%)
  other arithmetic  45.3 us (8%)
    psum x1, blocking collectives, body(): lax.psum((attn_gain_sum, mlp_gain_sum, query_gain_sum, key_gain_sum), BOTH)  94.1 us
    all_to_all x14, waiting for transfers between devices, exchange(): lax.all_to_all(blocks, axis, 0, 0, axis_index_groups=groups, tiled=True)  88.2 us
    all_to_all x14, starting transfers between devices, exchange(): lax.all_to_all(blocks, axis, 0, 0, axis_index_groups=groups, tiled=True)  81.5 us
    dot_general x29, matrix products, dot(): return lax.dot_general(a, b, (dims, ((), ())), preferred_element_type=F32)  53 us
    all_to_all x3, blocking collectives, exchange(): lax.all_to_all(blocks, axis, 0, 0, axis_index_groups=groups, tiled=True)  29.6 us
    unnamed x140, local copies, waits for them, and re-layouts  13.9 us
    reshape x4, local copies, waits for them, and re-layouts, scatter_sum(): parts = jnp.transpose(part.astype(BF).reshape(512, 2, 4, 128), (2, 0, 1, 3))  11.2 us
  transfers between devices with their start and end apart: 14, of which 8 were waited for; matrix products, arithmetic and copies ran while one was open for 28% of the time, Pallas kernels for 0%

profile of v1, /device:TPU:2, one launch (start us, length us, event | category | flops | bytes accessed | tf_op | source)
XLA Modules:
  0.0 545.0 jit_solution(2396641583294308032)
XLA Ops:
  3.5 8.0 %all-to-all-start.3 = ((s32[16,2,32]{2,1,0:T(2,128)}), s32[16,2,32]{2,1,0:T(2,128)S(1)}, u32[]{:S(2)}, u32[]{:S(2)}) async-start(s32[16,2,32]{2,1,0:T(2,128)} %copy.266), calls=%async_computation.3 | async-start | bytes 32768 | tf_op jit(solution)/shard_map/all_to_all | solution.py:49
  28.5 13.7 %all-to-all-done.1 = bf16[16,64,512]{2,1,0:T(8,128)(2,1)S(1)} async-done(((bf16[16,64,512]{2,1,0:T(8,128)(2,1)}), bf16[16,64,512]{2,1,0:T(8,128)(2,1)S(1)}, u32[]{:S(2)}, u32[]{:S(2)}) %all-to-all-start.1) | async-done | bytes 1048608 | tf_op jit(solution)/shard_map/all_to_all | solution.py:49
  42.5 5.4 all_to_all.85
  49.0 5.6 %all-to-all-start = ((bf16[128,32,128]{2,1,0:T(8,128)(2,1)}), bf16[128,32,128]{2,1,0:T(8,128)(2,1)S(1)}, u32[]{:S(2)}, u32[]{:S(2)}) async-start(bf16[128,32,128]{2,1,0:T(8,128)(2,1)} %bitcast.398), calls=%async_computation | async-start | bytes 2097152 | tf_op jit(solution)/shard_map/all_to_all | solution.py:49
  63.1 10.4 %all-to-all-done = bf16[128,32,128]{2,1,0:T(8,128)(2,1)S(1)} async-done(((bf16[128,32,128]{2,1,0:T(8,128)(2,1)}), bf16[128,32,128]{2,1,0:T(8,128)(2,1)S(1)}, u32[]{:S(2)}, u32[]{:S(2)}) %all-to-all-start) | async-done | bytes 1048608 | tf_op jit(solution)/shard_map/all_to_all | solution.py:49
  75.4 4.7 all-to-all-start.4
  91.4 33.0 %all-to-all-done.4 = bf16[16,64,1408]{2,1,0:T(8,128)(2,1)} async-done(((bf16[16,64,1408]{2,1,0:T(8,128)(2,1)}), bf16[16,64,1408]{2,1,0:T(8,128)(2,1)}, u32[]{:S(2)}, u32[]{:S(2)}) %all-to-all-start.4) | async-done | bytes 2883616 | tf_op jit(solution)/shard_map/all_to_all | solution.py:49
  127.0 9.6 %all_to_all.86 = bf16[2,16,64,1408]{3,2,1,0:T(8,128)(2,1)} all-to-all(bf16[2,16,64,1408]{3,2,1,0:T(8,128)(2,1)S(1)} %broadcast_in_dim.73), channel_id=1, replica_groups={{0,8},{16,24},{32,40},{48,56},{64,72},{80,88},{96,104},{112,120},{1,9},..., dimensions={0} | all-to-all | bytes 11534336 | tf_op jit(solution)/shard_map/all_to_all | solution.py:49
  137.7 6.4 %all-to-all-start.9 = ((bf16[128,32,128]{2,1,0:T(8,128)(2,1)}), bf16[128,32,128]{2,1,0:T(8,128)(2,1)S(1)}, u32[]{:S(2)}, u32[]{:S(2)}) async-start(bf16[128,32,128]{2,1,0:T(8,128)(2,1)} %bitcast.399), calls=%async_computation.9 | async-start | bytes 2097152 | tf_op jit(solution)/shard_map/all_to_all | solution.py:49
  164.8 5.3 all-to-all-start.6
  189.0 6.1 %all-to-all-start.7 = ((bf16[4,512,2,128]{3,2,1,0:T(2,128)(2,1)}), bf16[4,512,2,128]{3,2,1,0:T(2,128)(2,1)}, u32[]{:S(2)}, u32[]{:S(2)}) async-start(bf16[4,512,2,128]{3,2,1,0:T(2,128)(2,1)} %broadcast_in_dim.74), calls=%async_computation.7 | async-start | bytes 2097152 | tf_op jit(solution)/shard_map/all_to_all | solution.py:49
  246.0 5.0 all-to-all-start.10
  272.4 4.8 all-to-all-start.11
  327.3 5.0 all-to-all-start.13
  334.2 5.1 pad_maximum_fusion
  339.2 9.9 %all-to-all-start.8 = ((bf16[128,32,128]{2,1,0:T(8,128)(2,1)}), bf16[128,32,128]{2,1,0:T(8,128)(2,1)S(1)}, u32[]{:S(2)}, u32[]{:S(2)}) async-start(bf16[128,32,128]{2,1,0:T(8,128)(2,1)} %bitcast.400), calls=%async_computation.8 | async-start | bytes 2097152 | tf_op jit(solution)/shard_map/all_to_all | solution.py:49
  352.0 8.3 %copy.309 = bf16[1024,2,1408]{2,0,1:T(8,128)(2,1)} copy(bf16[1024,2,1408]{0,2,1:T(8,128)(2,1)} %pad_maximum_fusion) | data formatting | bytes 11534336 | tf_op jit(solution)/shard_map/concatenate | solution.py:237
  360.3 5.7 %copy.310 = bf16[2,8,2,64,1408]{4,3,1,2,0:T(8,128)(2,1)} copy(bf16[2,8,2,64,1408]{4,3,0,1,2:T(8,128)(2,1)} %bitcast.384) | data formatting | bytes 11534336 | tf_op jit(solution)/shard_map/convert_element_type | solution.py:72
  371.4 14.5 %all_to_all.87 = bf16[2,8,2,64,1408]{4,3,1,2,0:T(8,128)(2,1)} all-to-all(bf16[2,8,2,64,1408]{4,3,1,2,0:T(8,128)(2,1)} %copy.310), channel_id=1, replica_groups={{0,8},{16,24},{32,40},{48,56},{64,72},{80,88},{96,104},{112,120},{1,9},..., dimensions={0} | all-to-all | bytes 11534336 | tf_op jit(solution)/shard_map/all_to_all | solution.py:49
  385.9 7.7 %all-to-all-start.14 = ((bf16[16,64,512]{2,1,0:T(8,128)(2,1)}), bf16[16,64,512]{2,1,0:T(8,128)(2,1)S(1)}, u32[]{:S(2)}, u32[]{:S(2)}) async-start(bf16[16,64,512]{2,1,0:T(8,128)(2,1)} %bitcast.114), calls=%async_computation.14 | async-start | bytes 2097152 | tf_op jit(solution)/shard_map/all_to_all | solution.py:49
  399.9 11.5 %all-to-all-done.14 = bf16[16,64,512]{2,1,0:T(8,128)(2,1)S(1)} async-done(((bf16[16,64,512]{2,1,0:T(8,128)(2,1)}), bf16[16,64,512]{2,1,0:T(8,128)(2,1)S(1)}, u32[]{:S(2)}, u32[]{:S(2)}) %all-to-all-start.14) | async-done | bytes 1048608 | tf_op jit(solution)/shard_map/all_to_all | solution.py:49
  411.4 5.6 %all-to-all-start.12 = ((bf16[128,32,128]{2,1,0:T(8,128)(2,1)}), bf16[128,32,128]{2,1,0:T(8,128)(2,1)S(1)}, u32[]{:S(2)}, u32[]{:S(2)}) async-start(bf16[128,32,128]{2,1,0:T(8,128)(2,1)} %bitcast.97), calls=%async_computation.12 | async-start | bytes 2097152 | tf_op jit(solution)/shard_map/all_to_all | solution.py:49
  422.7 13.3 %all-to-all-done.12 = bf16[128,32,128]{2,1,0:T(8,128)(2,1)S(1)} async-done(((bf16[128,32,128]{2,1,0:T(8,128)(2,1)}), bf16[128,32,128]{2,1,0:T(8,128)(2,1)S(1)}, u32[]{:S(2)}, u32[]{:S(2)}) %all-to-all-start.12) | async-done | bytes 1048608 | tf_op jit(solution)/shard_map/all_to_all | solution.py:49
  443.8 94.1 %all-reduce = (f32[1024]{0:T(1024)}, f32[128]{0:T(128)}, f32[128]{0:T(128)}, f32[1024]{0:T(1024)}) all-reduce(f32[1024]{0:T(1024)S(1)} %get-tuple-element.15, f32[128]{0:T(128)S(1)} %get-tuple-element.17, f32[128]{0:T(128)S(1)} %get-tuple-element.19, f32[1024]{0:T(1024)S(1)} %get-tuple-element.13), channel_id=1, replica_groups=mesh['row'=16,'col'=8] {'row','col'}, use_global_device_ids=true, to_apply=%region_19.20 | all-reduce | flops 2304 | bytes 18432 | tf_op jit(solution)/shard_map/psum | solution.py:291
  (320 shorter events, 241.8 us)
Async XLA Ops:
  0.6 26.7 %copy-start = (s32[2,512]{1,0:T(2,128)S(1)}, s32[2,512]{1,0:T(2,128)}, u32[]{:S(2)}) copy-start(s32[2,512]{1,0:T(2,128)} %param.20) | copy-start | bytes 12292
  0.7 14.0 %copy-start.58 = (bf16[2,512,128]{2,1,0:T(8,128)(2,1)S(1)}, bf16[2,512,128]{2,1,0:T(8,128)(2,1)}, u32[]{:S(2)}) copy-start(bf16[2,512,128]{2,1,0:T(8,128)(2,1)} %param.17) | copy-start | bytes 786436
  3.5 15.6 %all-to-all-start.3 = ((s32[16,2,32]{2,1,0:T(2,128)}), s32[16,2,32]{2,1,0:T(2,128)S(1)}, u32[]{:S(2)}, u32[]{:S(2)}) async-start(s32[16,2,32]{2,1,0:T(2,128)} %copy.266), calls=%async_computation.3 | async-start | bytes 32768 | tf_op jit(solution)/shard_map/all_to_all | solution.py:49
  15.5 11.9 %copy-start.56 = (bf16[1024]{0:T(1024)(128)(2,1)S(1)}, bf16[1024]{0:T(1024)(128)(2,1)}, u32[]{:S(2)}) copy-start(bf16[1024]{0:T(1024)(128)(2,1)} %param.21) | copy-start | bytes 6148
  15.5 11.9 %copy-start.49 = (bf16[384,64]{0,1:T(8,128)(2,1)S(1)}, bf16[384,64]{0,1:T(8,128)(2,1)}, u32[]{:S(2)}) copy-start(bf16[384,64]{0,1:T(8,128)(2,1)} %param.31) | copy-start | bytes 147460
  15.5 11.9 %copy-start.50 = (bf16[64,384]{1,0:T(8,128)(2,1)S(1)}, bf16[64,384]{1,0:T(8,128)(2,1)}, u32[]{:S(2)}) copy-start(bf16[64,384]{1,0:T(8,128)(2,1)} %param.30) | copy-start | bytes 147460
  15.5 11.9 %copy-start.51 = (bf16[64,384]{1,0:T(8,128)(2,1)S(1)}, bf16[64,384]{1,0:T(8,128)(2,1)}, u32[]{:S(2)}) copy-start(bf16[64,384]{1,0:T(8,128)(2,1)} %param.29) | copy-start | bytes 147460
  15.6 11.9 %copy-start.53 = (bf16[256,64]{0,1:T(8,128)(2,1)S(1)}, bf16[256,64]{0,1:T(8,128)(2,1)}, u32[]{:S(2)}) copy-start(bf16[256,64]{0,1:T(8,128)(2,1)} %param.27) | copy-start | bytes 98308
  20.3 21.9 %all-to-all-start.1 = ((bf16[16,64,512]{2,1,0:T(8,128)(2,1)}), bf16[16,64,512]{2,1,0:T(8,128)(2,1)S(1)}, u32[]{:S(2)}, u32[]{:S(2)}) async-start(bf16[16,64,512]{2,1,0:T(8,128)(2,1)} %broadcast_in_dim.59), calls=%async_computation.1 | async-start | bytes 2097152 | tf_op jit(solution)/shard_map/all_to_all | solution.py:49
  49.0 24.5 %all-to-all-start = ((bf16[128,32,128]{2,1,0:T(8,128)(2,1)}), bf16[128,32,128]{2,1,0:T(8,128)(2,1)S(1)}, u32[]{:S(2)}, u32[]{:S(2)}) async-start(bf16[128,32,128]{2,1,0:T(8,128)(2,1)} %bitcast.398), calls=%async_computation | async-start | bytes 2097152 | tf_op jit(solution)/shard_map/all_to_all | solution.py:49
  60.7 12.8 %copy-start.44 = (bf16[64,1408]{1,0:T(8,128)(2,1)S(1)}, bf16[64,1408]{1,0:T(8,128)(2,1)}, u32[]{:S(2)}) copy-start(bf16[64,1408]{1,0:T(8,128)(2,1)} %pad_maximum_fusion.5) | copy-start | bytes 540676
  75.4 49.0 %all-to-all-start.4 = ((bf16[16,64,1408]{2,1,0:T(8,128)(2,1)}), bf16[16,64,1408]{2,1,0:T(8,128)(2,1)}, u32[]{:S(2)}, u32[]{:S(2)}) async-start(bf16[16,64,1408]{2,1,0:T(8,128)(2,1)} %broadcast_in_dim.72), calls=%async_computation.4 | async-start | bytes 5767168 | tf_op jit(solution)/shard_map/all_to_all | solution.py:49
  126.9 9.6 %copy-start.37 = (bf16[16,2,32,128]{3,2,1,0:T(8,128)(2,1)S(1)}, bf16[16,2,32,128]{3,2,1,0:T(8,128)(2,1)}, u32[]{:S(2)}) copy-start(bf16[16,2,32,128]{3,2,1,0:T(8,128)(2,1)} %copy.282) | copy-start | bytes 786436
  137.7 27.1 %all-to-all-start.9 = ((bf16[128,32,128]{2,1,0:T(8,128)(2,1)}), bf16[128,32,128]{2,1,0:T(8,128)(2,1)S(1)}, u32[]{:S(2)}, u32[]{:S(2)}) async-start(bf16[128,32,128]{2,1,0:T(8,128)(2,1)} %bitcast.399), calls=%async_computation.9 | async-start | bytes 2097152 | tf_op jit(solution)/shard_map/all_to_all | solution.py:49
  164.8 18.9 %all-to-all-start.6 = ((bf16[4,512,2,128]{3,2,1,0:T(2,128)(2,1)}), bf16[4,512,2,128]{3,2,1,0:T(2,128)(2,1)}, u32[]{:S(2)}, u32[]{:S(2)}) async-start(bf16[4,512,2,128]{3,2,1,0:T(2,128)(2,1)} %bitcast.403), calls=%async_computation.6 | async-start | bytes 2097152 | tf_op jit(solution)/shard_map/all_to_all | solution.py:49
  189.0 27.9 %all-to-all-start.7 = ((bf16[4,512,2,128]{3,2,1,0:T(2,128)(2,1)}), bf16[4,512,2,128]{3,2,1,0:T(2,128)(2,1)}, u32[]{:S(2)}, u32[]{:S(2)}) async-start(bf16[4,512,2,128]{3,2,1,0:T(2,128)(2,1)} %broadcast_in_dim.74), calls=%async_computation.7 | async-start | bytes 2097152 | tf_op jit(solution)/shard_map/all_to_all | solution.py:49
  246.0 21.2 %all-to-all-start.10 = ((bf16[4,512,2,128]{3,2,1,0:T(2,128)(2,1)}), bf16[4,512,2,128]{3,2,1,0:T(2,128)(2,1)}, u32[]{:S(2)}, u32[]{:S(2)}) async-start(bf16[4,512,2,128]{3,2,1,0:T(2,128)(2,1)} %bitcast.404), calls=%async_computation.10 | async-start | bytes 2097152 | tf_op jit(solution)/shard_map/all_to_all | solution.py:49
  272.4 16.4 %all-to-all-start.11 = ((bf16[4,512,2,128]{3,2,1,0:T(2,128)(2,1)}), bf16[4,512,2,128]{3,2,1,0:T(2,128)(2,1)}, u32[]{:S(2)}, u32[]{:S(2)}) async-start(bf16[4,512,2,128]{3,2,1,0:T(2,128)(2,1)} %broadcast_in_dim.78), calls=%async_computation.11 | async-start | bytes 2097152 | tf_op jit(solution)/shard_map/all_to_all | solution.py:49
  327.3 12.0 %all-to-all-start.13 = ((bf16[2,8,2,64,512]{4,3,1,2,0:T(8,128)(2,1)}), bf16[2,8,2,64,512]{4,3,1,2,0:T(8,128)(2,1)}, u32[]{:S(2)}, u32[]{:S(2)}) async-start(bf16[2,8,2,64,512]{4,3,1,2,0:T(8,128)(2,1)} %copy.301), calls=%async_computation.13 | async-start | bytes 4194304 | tf_op jit(solution)/shard_map/all_to_all | solution.py:49
  339.2 32.2 %all-to-all-start.8 = ((bf16[128,32,128]{2,1,0:T(8,128)(2,1)}), bf16[128,32,128]{2,1,0:T(8,128)(2,1)S(1)}, u32[]{:S(2)}, u32[]{:S(2)}) async-start(bf16[128,32,128]{2,1,0:T(8,128)(2,1)} %bitcast.400), calls=%async_computation.8 | async-start | bytes 2097152 | tf_op jit(solution)/shard_map/all_to_all | solution.py:49
  371.4 14.6 %copy-start.17 = (bf16[128,32,128]{2,1,0:T(8,128)(2,1)}, bf16[128,32,128]{2,1,0:T(8,128)(2,1)S(1)}, u32[]{:S(2)}) copy-start(bf16[128,32,128]{2,1,0:T(8,128)(2,1)S(1)} %all-to-all-done.8) | copy-start | bytes 3145732
  385.9 25.5 %all-to-all-start.14 = ((bf16[16,64,512]{2,1,0:T(8,128)(2,1)}), bf16[16,64,512]{2,1,0:T(8,128)(2,1)S(1)}, u32[]{:S(2)}, u32[]{:S(2)}) async-start(bf16[16,64,512]{2,1,0:T(8,128)(2,1)} %bitcast.114), calls=%async_computation.14 | async-start | bytes 2097152 | tf_op jit(solution)/shard_map/all_to_all | solution.py:49
  411.4 24.5 %all-to-all-start.12 = ((bf16[128,32,128]{2,1,0:T(8,128)(2,1)}), bf16[128,32,128]{2,1,0:T(8,128)(2,1)S(1)}, u32[]{:S(2)}, u32[]{:S(2)}) async-start(bf16[128,32,128]{2,1,0:T(8,128)(2,1)} %bitcast.97), calls=%async_computation.12 | async-start | bytes 2097152 | tf_op jit(solution)/shard_map/all_to_all | solution.py:49
  436.9 105.9 %all-to-all-start.16 = ((bf16[16,64,1408]{2,1,0:T(8,128)(2,1)}), bf16[16,64,1408]{2,1,0:T(8,128)(2,1)S(1)}, u32[]{:S(2)}, u32[]{:S(2)}) async-start(bf16[16,64,1408]{2,1,0:T(8,128)(2,1)} %bitcast.128), calls=%async_computation.16 | async-start | bytes 5767168 | tf_op jit(solution)/shard_map/all_to_all | solution.py:49
  (59 other events, 179.5 us)
